TPU v7x, 256 devices: a whole 4x4x8 slice. The times are simulated.
256 devices in a mesh: dp: 4 (over x), seq: 64 (over y, z, core).
Axes of the slice: x: 4, y: 4, z: 8, core: 2. Of those that a mesh axis runs over, the one named last changes fastest.
Arguments:
- tokens: bfloat16 [4, 8192, 2048], P('dp', 'seq'), may hold values from -6 to 6
- values: bfloat16 [4, 8192, 1024], P('dp', 'seq'), may hold values from -6 to 6
- cotangent: bfloat16 [4, 8192, 1024], P('dp', 'seq'), may hold values from -6 to 6
- sel_weight: bfloat16 [2048, 128], P(('dp', 'seq')), may hold values from -0.03125 to 0.03125
- step_weight: bfloat16 [2048, 32], P(('dp', 'seq')), may hold values from -0.125 to 0.125
- sel_dir: bfloat16 [2048, 128], P(('dp', 'seq')), may hold values from -0.03125 to 0.03125
- step_dir: bfloat16 [2048, 32], P(('dp', 'seq')), may hold values from -0.125 to 0.125
- conv_weight: float32 [4, 128], replicated, may hold values from -3 to 3
- step_bias: float32 [32], replicated, may hold values from -1 to 0.5
- decay_rate: float32 [32], replicated, may hold values from 0 to 1
Outputs:
- sel_grad: float32 [2048, 128], P(('dp', 'seq'))
- step_grad: float32 [2048, 32], P(('dp', 'seq'))
- sel_hvp: float32 [2048, 128], P(('dp', 'seq'))
- step_hvp: float32 [2048, 32], P(('dp', 'seq'))
All inputs are finite; a program needn't handle non-finite values.
Results may differ from a plain program's by a relative error of at most 0.0003.
Values may be sent and summed in bfloat16 or wider, within the bound.
A program may use at most 192 MiB of HBM per device.

v0:
```python
import math
import jax
import jax.numpy as jnp
from jax import lax
from jax.sharding import PartitionSpec as P

N = 64
P_SIZE = 32
H = 32
KCONV = 4
HIGHEST = lax.Precision.HIGHEST


def shifted(value, axis, steps):
    count = lax.axis_size(axis)
    initial, last = (max(0, -steps), min(count, count - steps))
    return lax.ppermute(value, axis, [(source, source + steps) for source in range(initial, last)])


def prefix(part, axis, combine, identity, reverse):
    count = lax.axis_size(axis)
    place = lax.axis_index(axis)
    ahead = count - 1 - place if reverse else place
    gathered = jax.tree.map(lambda a: lax.all_gather(a, axis), part)
    state = jax.tree.map(lambda a, e: jnp.zeros_like(a) + jnp.asarray(e, a.dtype), part, identity)

    def one(turn, state):
        source = count - 1 - turn if reverse else turn
        return combine(
            state, jax.tree.map(lambda a: lax.dynamic_index_in_dim(a, source, 0, False), gathered)
        )

    return lax.fori_loop(0, ahead, one, state)


def state_space(in_map, out_map, step_size, head_values, decay_rate, state_in):
    cumulated = jnp.cumsum(-step_size * decay_rate[None, :], axis=0)
    cumulated_heads = cumulated.T
    spans = cumulated_heads[:, :, None] - cumulated_heads[:, None, :]
    length = in_map.shape[0]
    causal = jnp.arange(length)[:, None] >= jnp.arange(length)[None, :]
    decays = jnp.exp(jnp.where(causal[None], spans, -1e30))
    intersection = jnp.dot(out_map, in_map.T, precision=HIGHEST)
    mixing = decays * intersection[None] * step_size.T[:, None, :]
    within = jnp.einsum("hts,shp->thp", mixing, head_values, precision=HIGHEST)
    carried = jnp.exp(cumulated)[:, :, None] * jnp.einsum(
        "tn,hpn->thp", out_map, state_in, precision=HIGHEST
    )
    whole_decay = cumulated[-1]
    tail_weight = jnp.exp(whole_decay[None, :] - cumulated) * step_size
    local_state = jnp.einsum(
        "thp,tn->hpn", head_values * tail_weight[:, :, None], in_map, precision=HIGHEST
    )
    state_out = jnp.exp(whole_decay)[:, None, None] * state_in + local_state
    return (within + carried, state_out)


def features(sel_float, step_float, extended, conv_weight, step_bias, length):
    projected = jnp.dot(extended, sel_float, precision=HIGHEST)
    convolved = conv_weight[0][None, :] * projected[0:length]
    for offset in range(1, KCONV):
        convolved = convolved + conv_weight[offset][None, :] * projected[offset : offset + length]
    activated = jax.nn.silu(convolved)
    step_size = jax.nn.softplus(
        jnp.dot(extended[KCONV - 1 :], step_float, precision=HIGHEST) + step_bias[None, :]
    )
    return (activated[:, :N], activated[:, N:], step_size)


def combine(earlier_segment, later_segment):
    decay_first, state_first, tangent_decay_first, tangent_state_first = earlier_segment
    decay_second, state_second, tangent_decay_second, tangent_state_second = later_segment
    combined_decay = decay_first * decay_second
    combined_state = decay_second[:, None, None] * state_first + state_second
    tangent_decay_combined = tangent_decay_first * decay_second + decay_first * tangent_decay_second
    tangent_state_combined = (
        tangent_decay_second[:, None, None] * state_first
        + decay_second[:, None, None] * tangent_state_first
        + tangent_state_second
    )
    return (combined_decay, combined_state, tangent_decay_combined, tangent_state_combined)


def body(
    tokens,
    values,
    cotangent,
    sel_weight,
    step_weight,
    sel_dir,
    step_dir,
    conv_weight,
    step_bias,
    decay_rate,
):
    own_tokens = tokens[0]
    length = own_tokens.shape[0]
    head_values = values[0].reshape(length, H, P_SIZE).astype(jnp.float32)
    head_cotangent = cotangent[0].reshape(length, H, P_SIZE).astype(jnp.float32)
    gathered = (
        lax.all_gather(sel_weight, ("dp", "seq"), axis=0, tiled=True),
        lax.all_gather(step_weight, ("dp", "seq"), axis=0, tiled=True),
        lax.all_gather(sel_dir, ("dp", "seq"), axis=0, tiled=True),
        lax.all_gather(step_dir, ("dp", "seq"), axis=0, tiled=True),
    )
    parameters = (gathered[0].astype(jnp.float32), gathered[1].astype(jnp.float32))
    directions = (gathered[2].astype(jnp.float32), gathered[3].astype(jnp.float32))
    previous = shifted(own_tokens[length - (KCONV - 1) :], "seq", 1)
    extended = jnp.concatenate([previous, own_tokens], axis=0).astype(jnp.float32)
    token_count = lax.axis_size("dp") * lax.axis_size("seq") * length
    scale_factor = 1.0 / math.sqrt(token_count)

    def summaries(weights):
        in_map, out_map, step_size = features(
            weights[0], weights[1], extended, conv_weight, step_bias, length
        )
        cumulated = jnp.cumsum(-step_size * decay_rate[None, :], axis=0)
        whole_decay = cumulated[-1]
        tail_weight = jnp.exp(whole_decay[None, :] - cumulated) * step_size
        local_state = jnp.einsum(
            "thp,tn->hpn", head_values * tail_weight[:, :, None], in_map, precision=HIGHEST
        )
        local_adjoint = scale_factor * jnp.einsum(
            "thp,tn->hpn",
            head_cotangent * jnp.exp(cumulated)[:, :, None],
            out_map,
            precision=HIGHEST,
        )
        return (jnp.exp(whole_decay), local_state, local_adjoint)

    primal, tangent = jax.jvp(summaries, (parameters,), (directions,))
    identity = (
        jnp.ones((H,), jnp.float32),
        jnp.zeros((H, P_SIZE, N), jnp.float32),
        jnp.zeros((H,), jnp.float32),
        jnp.zeros((H, P_SIZE, N), jnp.float32),
    )
    forward = prefix(
        (primal[0], primal[1], tangent[0], tangent[1]), "seq", combine, identity, False
    )
    backward = prefix(
        (primal[0], primal[2], tangent[0], tangent[2]), "seq", combine, identity, True
    )

    def objective(weights, state_start, end_adjoint):
        in_map, out_map, step_size = features(
            weights[0], weights[1], extended, conv_weight, step_bias, length
        )
        outputs, state_end = state_space(
            in_map, out_map, step_size, head_values, decay_rate, state_start
        )
        return scale_factor * jnp.sum(head_cotangent * outputs) + jnp.sum(end_adjoint * state_end)

    local_gradient = jax.grad(objective)
    gradients, curvature = jax.jvp(
        local_gradient, (parameters, forward[1], backward[1]), (directions, forward[3], backward[3])
    )
    reduced = (
        lax.psum_scatter(gradients[0], ("dp", "seq"), scatter_dimension=0, tiled=True),
        lax.psum_scatter(gradients[1], ("dp", "seq"), scatter_dimension=0, tiled=True),
        lax.psum_scatter(curvature[0], ("dp", "seq"), scatter_dimension=0, tiled=True),
        lax.psum_scatter(curvature[1], ("dp", "seq"), scatter_dimension=0, tiled=True),
    )
    return (reduced[0], reduced[1], reduced[2], reduced[3])


def solution(mesh):
    return jax.shard_map(
        body,
        mesh=mesh,
        in_specs=(
            P("dp", "seq", None),
            P("dp", "seq", None),
            P("dp", "seq", None),
            P(("dp", "seq"), None),
            P(("dp", "seq"), None),
            P(("dp", "seq"), None),
            P(("dp", "seq"), None),
            P(),
            P(),
            P(),
        ),
        out_specs=(
            P(("dp", "seq"), None),
            P(("dp", "seq"), None),
            P(("dp", "seq"), None),
            P(("dp", "seq"), None),
        ),
        check_vma=False,
    )
```

profile of v0, /device:TPU:8, one launch (start us, length us, event | category | flops | bytes accessed | tf_op | source)
XLA Modules:
  0.0 1398.3 jit_solution(11636096432629976415)
XLA Ops:
  8.1 1.9 collective-permute-start
  10.0 71.2 %all_gather.55 = bf16[2048,128]{1,0:T(8,128)(2,1)S(1)} all-gather(bf16[8,128]{1,0:T(8,128)(2,1)} %param.19), channel_id=1, replica_groups=mesh['dp'=4,'seq'=64] {'dp','seq'}, dimensions={0}, use_global_device_ids=true | all-gather | bytes 526336 | tf_op jit(solution)/shard_map/all_gather | solution.py:103
  81.2 65.5 %all_gather.50 = bf16[2048,128]{1,0:T(8,128)(2,1)S(1)} all-gather(bf16[8,128]{1,0:T(8,128)(2,1)} %param.17), channel_id=1, replica_groups=mesh['dp'=4,'seq'=64] {'dp','seq'}, dimensions={0}, use_global_device_ids=true | all-gather | bytes 526336 | tf_op jit(solution)/shard_map/all_gather | solution.py:101
  146.7 65.6 %all_gather.48 = bf16[2048,32]{1,0:T(8,128)(2,1)S(1)} all-gather(bf16[8,32]{1,0:T(8,128)(2,1)} %param.18), channel_id=1, replica_groups=mesh['dp'=4,'seq'=64] {'dp','seq'}, dimensions={0}, use_global_device_ids=true | all-gather | bytes 131584 | tf_op jit(solution)/shard_map/all_gather | solution.py:102
  212.3 65.5 %all_gather.53 = bf16[2048,32]{1,0:T(8,128)(2,1)S(1)} all-gather(bf16[8,32]{1,0:T(8,128)(2,1)} %param.20), channel_id=1, replica_groups=mesh['dp'=4,'seq'=64] {'dp','seq'}, dimensions={0}, use_global_device_ids=true | all-gather | bytes 131584 | tf_op jit(solution)/shard_map/all_gather | solution.py:104
  285.1 37.7 %all-gather.4 = f32[64,1,32]{2,1,0:T(1,128)S(1)} all-gather(f32[1,1,32]{2,1,0:T(1,128)S(1)} %get-tuple-element.315), channel_id=1, replica_groups=mesh['dp'=4,'seq'=64] {'seq'}, dimensions={0}, use_global_device_ids=true | all-gather | bytes 8320 | tf_op jit(solution)/shard_map/all_gather | solution.py:24
  322.8 38.1 %all-gather.5 = f32[64,1,32]{2,1,0:T(1,128)S(1)} all-gather(f32[1,1,32]{2,1,0:T(1,128)S(1)} %get-tuple-element.313), channel_id=1, replica_groups=mesh['dp'=4,'seq'=64] {'seq'}, dimensions={0}, use_global_device_ids=true | all-gather | bytes 8320 | tf_op jit(solution)/shard_map/all_gather | solution.py:24
  360.9 61.1 %all-gather.17.cloned.1.call-done = f32[2048,32,64]{2,1,0:T(8,128)} async-done(((f32[32,32,64]{2,1,0:T(8,128)}), f32[2048,32,64]{2,1,0:T(8,128)}) %all-gather.17.cloned.1.call-update) | async-done | bytes 16777232 | tf_op jit(solution)/shard_map/all_gather | solution.py:24
  422.0 142.3 %all-gather.15.cloned.1.call-done = f32[2048,32,64]{2,1,0:T(8,128)} async-done(((f32[32,32,64]{2,1,0:T(8,128)}), f32[2048,32,64]{2,1,0:T(8,128)}) %all-gather.15.cloned.1.call-update) | async-done | bytes 16777232 | tf_op jit(solution)/shard_map/all_gather | solution.py:24
  564.5 81.3 %while.33 = (s32[]{:T(128)}, f32[32,32,64]{2,1,0:T(8,128)S(1)}, f32[32,32,64]{2,1,0:T(8,128)S(1)}, s32[]{:T(128)}, f32[64,32]{1,0:T(8,128)S(1)}, /*index=5*/f32[...) while((s32[]{:T(128)}, f32[32,32,64]{2,1,0:T(8,128)S(1)}, ...), condition=%wide.region_6.7_spmd, body=%wide.region_5.6_spmd.sunk | while | flops 393222 | bytes 1573803 | solution.py:33
  564.5 1.7 bitcast_add_fusion.13
  566.2 1.7 bitcast_add_fusion.13
  568.0 1.7 bitcast_add_fusion.13
  569.7 1.7 bitcast_add_fusion.13
  571.4 1.7 bitcast_add_fusion.13
  573.1 1.7 bitcast_add_fusion.13
  574.9 1.7 bitcast_add_fusion.13
  576.6 1.7 bitcast_add_fusion.13
  578.3 1.7 bitcast_add_fusion.13
  580.0 1.7 bitcast_add_fusion.13
  581.8 1.7 bitcast_add_fusion.13
  583.5 1.7 bitcast_add_fusion.13
  585.2 1.7 bitcast_add_fusion.13
  586.9 1.7 bitcast_add_fusion.13
  588.7 1.7 bitcast_add_fusion.13
  590.4 1.7 bitcast_add_fusion.13
  592.1 1.7 bitcast_add_fusion.13
  593.8 1.7 bitcast_add_fusion.13
  595.6 1.7 bitcast_add_fusion.13
  597.3 1.7 bitcast_add_fusion.13
  600.8 1.7 bitcast_add_fusion.13
  604.2 1.7 bitcast_add_fusion.13
  612.8 1.7 bitcast_add_fusion.13
  616.3 1.7 bitcast_add_fusion.13
  619.7 1.7 bitcast_add_fusion.13
  623.2 1.7 bitcast_add_fusion.13
  626.6 1.7 bitcast_add_fusion.13
  630.1 1.7 bitcast_add_fusion.13
  633.5 1.7 bitcast_add_fusion.13
  637.0 1.7 bitcast_add_fusion.13
  655.5 5.9 fusion.150
  671.4 144.6 %all-gather.13.cloned.1.call-done = f32[2048,32,64]{2,1,0:T(8,128)} async-done(((f32[32,32,64]{2,1,0:T(8,128)}), f32[2048,32,64]{2,1,0:T(8,128)}) %all-gather.13.cloned.1.call-update) | async-done | bytes 16777232 | tf_op jit(solution)/shard_map/all_gather | solution.py:24
  816.0 142.2 %all-gather.11.cloned.1.call-done = f32[2048,32,64]{2,1,0:T(8,128)} async-done(((f32[32,32,64]{2,1,0:T(8,128)}), f32[2048,32,64]{2,1,0:T(8,128)}) %all-gather.11.cloned.1.call-update) | async-done | bytes 16777232 | tf_op jit(solution)/shard_map/all_gather | solution.py:24
  958.3 38.5 %while.32 = (s32[]{:T(128)}, f32[32,32,64]{2,1,0:T(8,128)S(1)}, f32[32,32,64]{2,1,0:T(8,128)S(1)}, s32[]{:T(128)}, f32[64,32]{1,0:T(8,128)}, /*index=5*/f32[64,3...) while((s32[]{:T(128)}, f32[32,32,64]{2,1,0:T(8,128)S(1)}, ...), condition=%wide.region_3.4_spmd, body=%wide.region_2.3_spmd.sunk | while | flops 393221 | bytes 1573783 | solution.py:33
  1001.1 1.8 convolution_bitcast_fusion.5
  1010.8 2.3 fusion.42
  1013.1 2.3 fusion.50
  1015.4 373.0 %all-reduce.21.cloned.1.call-done = (f32[2048,128]{1,0:T(8,128)}, f32[2048,32]{0,1:T(8,128)}, f32[2048,128]{1,0:T(8,128)}, f32[2048,32]{0,1:T(8,128)}) async-done(((f32[2048,128]{1,0:T(8,128)}, f32[2048,32]{0,1:T(8,128)}, f32[2048,128]{1,0:T(8,128)}, f32[2048,32]{0,1:T(8,128)}), (f32[2048,128]{1,0:T(8,128)}, f32[2048,32]{0,1:T(8,128)}, f32[2048,128]{1,0:T(8,128)}, ...) | async-done | bytes 2621456
  (281 shorter events, 109.8 us)
Async XLA Ops:
  7.2 270.6 %copy-start = (bf16[1,128,2048]{2,1,0:T(8,128)(2,1)S(1)}, bf16[1,128,2048]{2,1,0:T(8,128)(2,1)}, u32[]{:S(2)}) copy-start(bf16[1,128,2048]{2,1,0:T(8,128)(2,1)} %param.14) | copy-start | bytes 1572868
  7.2 270.6 %copy-start.46 = (f32[32]{0:T(128)S(1)}, f32[32]{0:T(128)}, u32[]{:S(2)}) copy-start(f32[32]{0:T(128)} %param.22) | copy-start | bytes 388
  7.2 270.9 %copy-start.29 = (f32[32]{0:T(128)S(1)}, f32[32]{0:T(128)}, u32[]{:S(2)}) copy-start(f32[32]{0:T(128)} %param.23) | copy-start | bytes 388
  7.2 414.8 %all-gather.17.cloned.1.call-start = ((), (), s32[]{:S(2)}) async-start(), calls=%async_computation.3 | async-start | bytes 34078720 | tf_op jit(solution)/shard_map/all_gather | solution.py:24
  8.1 271.7 %collective-permute-start = (bf16[3,2048]{1,0:T(4,128)(2,1)S(1)}, bf16[3,2048]{1,0:T(4,128)(2,1)S(1)}, u32[]{:S(2)}, u32[]{:S(2)}) collective-permute-start(bf16[3,2048]{1,0:T(4,128)(2,1)S(1)} %slice_bitcast_fusion), channel_id=1, source_target_pairs={{0,1},{1,2},{2,3},{3,4},{4,5},{5,6},{6,7},{7,8},{8,9},{9,10},{10,1... | collective-permute-start | bytes 36872 | tf_op jit(solution)/shard_map/ppermute | solution.py:17
  146.7 132.7 %copy-start.43 = (f32[4,128]{1,0:T(4,128)S(1)}, f32[4,128]{1,0:T(4,128)}, u32[]{:S(2)}) copy-start(f32[4,128]{1,0:T(4,128)} %param.21) | copy-start | bytes 6148
  146.7 132.8 %copy-start.12 = (bf16[1,128,1024]{2,1,0:T(8,128)(2,1)S(1)}, bf16[1,128,1024]{2,1,0:T(8,128)(2,1)}, u32[]{:S(2)}) copy-start(bf16[1,128,1024]{2,1,0:T(8,128)(2,1)} %param.16) | copy-start | bytes 786436
  278.4 375.1 %copy-start.1 = (f32[128,32]{1,0:T(8,128)}, f32[128,32]{1,0:T(8,128)S(1)}, u32[]{:S(2)}) copy-start(f32[128,32]{1,0:T(8,128)S(1)} %get-tuple-element.326) | copy-start | bytes 49156
  279.4 2.0 copy-start.8
  279.4 2.0 copy-start.33
  281.4 3.4 copy-start.10
  282.0 2.9 copy-start.15
  283.4 280.9 %all-gather.15.cloned.1.call-start = ((), (), s32[]{:S(2)}) async-start(), calls=%async_computation.2 | async-start | bytes 34078720 | tf_op jit(solution)/shard_map/all_gather | solution.py:24
  284.8 531.2 %all-gather.13.cloned.1.call-start = ((), (), s32[]{:S(2)}) async-start(), calls=%async_computation.1 | async-start | bytes 34078720 | tf_op jit(solution)/shard_map/all_gather | solution.py:24
  285.1 362.7 %copy-start.27 = (f32[32]{0:T(128)}, f32[32]{0:T(128)S(1)}, u32[]{:S(2)}) copy-start(f32[32]{0:T(128)S(1)} %get-tuple-element.314) | copy-start | bytes 388
  285.1 362.7 %copy-start.31 = (f32[32]{0:T(128)}, f32[32]{0:T(128)S(1)}, u32[]{:S(2)}) copy-start(f32[32]{0:T(128)S(1)} %get-tuple-element.312) | copy-start | bytes 388
  647.7 5.8 copy-start.5
  649.7 4.2 copy-start.13
  652.1 306.1 %all-gather.11.cloned.1.call-start = ((), (), s32[]{:S(2)}) async-start(), calls=%async_computation | async-start | bytes 34078720 | tf_op jit(solution)/shard_map/all_gather | solution.py:24
  653.5 734.9 %all-reduce.21.cloned.1.call-start = ((), (), s32[]{:S(2)}) async-start(), calls=%async_computation.4 | async-start | bytes 5242880
  661.4 296.8 %copy-start.3 = (f32[128,128]{1,0:T(8,128)}, f32[128,128]{1,0:T(8,128)S(1)}, u32[]{:S(2)}) copy-start(f32[128,128]{1,0:T(8,128)S(1)} %get-tuple-element.236) | copy-start | bytes 196612
  999.5 3.4 copy-start.41
  999.5 3.4 copy-start.42
  999.5 3.4 copy-start.44
  999.5 3.4 copy-start.45
  999.5 3.4 copy-start.9
  999.5 3.5 copy-start.17
  999.5 3.5 copy-start.18
  999.5 3.5 copy-start.19
  999.5 3.5 copy-start.20
  999.5 3.5 copy-start.21
  999.5 3.5 copy-start.28
  1001.1 4.3 copy-start.4
  1002.8 5.0 copy-start.7
  1002.8 5.0 copy-start.30
  1003.1 5.9 copy-start.2
  1003.1 5.9 copy-start.6
  1003.1 5.9 copy-start.14
  1003.1 5.9 copy-start.32
  1004.2 6.0 copy-start.24
  1004.2 6.3 copy-start.11
  1004.3 6.3 copy-start.16
  1004.3 6.3 copy-start.22
  1004.3 6.3 copy-start.23
  1004.3 6.3 copy-start.40
  1005.3 5.3 copy-start.34
  1005.3 5.3 copy-start.36
  1005.4 5.3 copy-start.38
  (5 other events, 7.6 us)
Sparse Core Ops, SparseCore 0:
  283.5 138.4 all-gather.16
  424.8 139.4 all-gather.14
  652.2 163.7 all-gather.12
  818.6 139.4 all-gather.10
  1015.6 372.8 all-reduce.20
where the time goes:
time: 1400 us
  waiting for transfers between devices  863 us (62%)
  blocking collectives  344 us (25%)
  other arithmetic  112 us (8%)
  matrix products  35.7 us (3%)
  local copies, waits for them, and re-layouts  24.1 us (2%)
  between operations  14.7 us (1%)
    all_gather x4, waiting for transfers between devices, prefix(): gathered = jax.tree.map(lambda a: lax.all_gather(a, axis), part)  490 us
    unnamed x6, waiting for transfers between devices  373 us
    add x63, other arithmetic, combine(): tangent_decay_second[:, None, None] * state_first  106 us
    all_gather x2, blocking collectives, prefix(): gathered = jax.tree.map(lambda a: lax.all_gather(a, axis), part)  75.8 us
    all_gather x1, blocking collectives, body(): lax.all_gather(sel_dir, ('dp', 'seq'), axis=0, tiled=True)  71.2 us
    all_gather x1, blocking collectives, body(): lax.all_gather(step_weight, ('dp', 'seq'), axis=0, tiled=True)  65.6 us
    all_gather x1, blocking collectives, body(): lax.all_gather(sel_weight, ('dp', 'seq'), axis=0, tiled=True)  65.5 us
    all_gather x1, blocking collectives, body(): lax.all_gather(step_dir, ('dp', 'seq'), axis=0, tiled=True)  65.5 us
  transfers between devices with their start and end apart: 6, of which 5 were waited for; matrix products, arithmetic and copies ran while one was open for 2% of the time, Pallas kernels for 0%

commit v1 on v0

--- a/solution.py
+++ b/solution.py
@@ -99,7 +99,12 @@
     head_cotangent = cotangent[0].reshape(length, H, P_SIZE).astype(jnp.float32)
     gathered = (
         lax.all_gather(sel_weight, ("dp", "seq"), axis=0, tiled=True),
-        lax.all_gather(step_weight, ("dp", "seq"), axis=0, tiled=True),
+        jnp.concatenate(
+            lax.all_to_all(
+                jnp.stack([step_weight] * lax.axis_size(("dp", "seq"))), ("dp", "seq"), 0, 0
+            ),
+            axis=0,
+        ),
         lax.all_gather(sel_dir, ("dp", "seq"), axis=0, tiled=True),
         lax.all_gather(step_dir, ("dp", "seq"), axis=0, tiled=True),
     )

time: 1400 us -> 1350 us (0.964)
  blocking collectives: 344 us -> 277 us
  starting transfers between devices: 2.13 us -> 17.5 us
    all_gather x1 -> x0, blocking collectives: 65.6 us -> none  [body(): lax.all_gather(step_weight, ('dp', 'seq'), axis=0, tiled=True)]
    all_to_all x0 -> x1, starting transfers between devices: none -> 15.3 us  [body(): lax.all_to_all(jnp.stack([step_weight] * lax.axis_size(('dp', 'seq'))), (...]
  transfers between devices with their start and end apart: 6 -> 7, of which waited for: 5 -> 5; matrix products, arithmetic and copies ran while one was open for 2% -> 2% of each run, Pallas kernels for 0% -> 0%
where the time goes in v1:
time: 1350 us
  waiting for transfers between devices  864 us (64%)
  blocking collectives  277 us (21%)
  other arithmetic  112 us (8%)
  matrix products  35.8 us (3%)
  local copies, waits for them, and re-layouts  26 us (2%)
  starting transfers between devices  17.5 us (1%)
  between operations  14.7 us (1%)
    all_gather x4, waiting for transfers between devices, prefix(): gathered = jax.tree.map(lambda a: lax.all_gather(a, axis), part)  491 us
    unnamed x6, waiting for transfers between devices  373 us
    add x63, other arithmetic, combine(): tangent_decay_second[:, None, None] * state_first  106 us
    all_gather x2, blocking collectives, prefix(): gathered = jax.tree.map(lambda a: lax.all_gather(a, axis), part)  75.8 us
    all_gather x1, blocking collectives, body(): lax.all_gather(sel_dir, ('dp', 'seq'), axis=0, tiled=True)  69.7 us
    all_gather x1, blocking collectives, body(): lax.all_gather(step_dir, ('dp', 'seq'), axis=0, tiled=True)  65.6 us
    all_gather x1, blocking collectives, body(): lax.all_gather(sel_weight, ('dp', 'seq'), axis=0, tiled=True)  65.5 us
  transfers between devices with their start and end apart: 7, of which 5 were waited for; matrix products, arithmetic and copies ran while one was open for 2% of the time, Pallas kernels for 0%

profile of v1, /device:TPU:8, one launch (start us, length us, event | category | flops | bytes accessed | tf_op | source)
XLA Modules:
  0.0 1348.8 jit_solution(12054182434155826631)
XLA Ops:
  8.0 1.9 collective-permute-start
  11.7 15.3 %all-to-all-start = ((bf16[256,2,128]{2,1,0:T(2,128)(2,1)}), bf16[256,2,128]{2,1,0:T(2,128)(2,1)S(1)}, u32[]{:S(2)}, u32[]{:S(2)}) async-start(bf16[256,2,128]{2,1,0:T(2,128)(2,1)} %reshape.135), calls=%async_computation | async-start | bytes 262144 | tf_op jit(solution)/shard_map/all_to_all | solution.py:103
  27.0 69.7 %all_gather.51 = bf16[2048,128]{1,0:T(8,128)(2,1)S(1)} all-gather(bf16[8,128]{1,0:T(8,128)(2,1)} %param.19), channel_id=1, replica_groups=mesh['dp'=4,'seq'=64] {'dp','seq'}, dimensions={0}, use_global_device_ids=true | all-gather | bytes 526336 | tf_op jit(solution)/shard_map/all_gather | solution.py:108
  96.7 65.5 %all_gather.46 = bf16[2048,128]{1,0:T(8,128)(2,1)S(1)} all-gather(bf16[8,128]{1,0:T(8,128)(2,1)} %param.17), channel_id=1, replica_groups=mesh['dp'=4,'seq'=64] {'dp','seq'}, dimensions={0}, use_global_device_ids=true | all-gather | bytes 526336 | tf_op jit(solution)/shard_map/all_gather | solution.py:101
  162.3 65.6 %all_gather.49 = bf16[2048,32]{1,0:T(8,128)(2,1)S(1)} all-gather(bf16[8,32]{1,0:T(8,128)(2,1)S(1)} %copy-done.40), channel_id=1, replica_groups=mesh['dp'=4,'seq'=64] {'dp','seq'}, dimensions={0}, use_global_device_ids=true | all-gather | bytes 131584 | tf_op jit(solution)/shard_map/all_gather | solution.py:109
  234.9 38.1 %all-gather.4 = f32[64,1,32]{2,1,0:T(1,128)S(1)} all-gather(f32[1,1,32]{2,1,0:T(1,128)S(1)} %get-tuple-element.315), channel_id=1, replica_groups=mesh['dp'=4,'seq'=64] {'seq'}, dimensions={0}, use_global_device_ids=true | all-gather | bytes 8320 | tf_op jit(solution)/shard_map/all_gather | solution.py:24
  273.0 37.6 %all-gather.5 = f32[64,1,32]{2,1,0:T(1,128)S(1)} all-gather(f32[1,1,32]{2,1,0:T(1,128)S(1)} %get-tuple-element.313), channel_id=1, replica_groups=mesh['dp'=4,'seq'=64] {'seq'}, dimensions={0}, use_global_device_ids=true | all-gather | bytes 8320 | tf_op jit(solution)/shard_map/all_gather | solution.py:24
  310.7 61.5 %all-gather.17.cloned.1.call-done = f32[2048,32,64]{2,1,0:T(8,128)} async-done(((f32[32,32,64]{2,1,0:T(8,128)}), f32[2048,32,64]{2,1,0:T(8,128)}) %all-gather.17.cloned.1.call-update) | async-done | bytes 16777232 | tf_op jit(solution)/shard_map/all_gather | solution.py:24
  372.2 142.3 %all-gather.15.cloned.1.call-done = f32[2048,32,64]{2,1,0:T(8,128)} async-done(((f32[32,32,64]{2,1,0:T(8,128)}), f32[2048,32,64]{2,1,0:T(8,128)}) %all-gather.15.cloned.1.call-update) | async-done | bytes 16777232 | tf_op jit(solution)/shard_map/all_gather | solution.py:24
  514.7 81.3 %while.33 = (s32[]{:T(128)}, f32[32,32,64]{2,1,0:T(8,128)S(1)}, f32[32,32,64]{2,1,0:T(8,128)S(1)}, s32[]{:T(128)}, f32[64,32]{1,0:T(8,128)S(1)}, /*index=5*/f32[...) while((s32[]{:T(128)}, f32[32,32,64]{2,1,0:T(8,128)S(1)}, ...), condition=%wide.region_6.7_spmd, body=%wide.region_5.6_spmd.sunk | while | flops 393222 | bytes 1573803 | solution.py:33
  514.7 1.7 bitcast_add_fusion.13
  516.4 1.7 bitcast_add_fusion.13
  518.2 1.7 bitcast_add_fusion.13
  519.9 1.7 bitcast_add_fusion.13
  521.6 1.7 bitcast_add_fusion.13
  523.3 1.7 bitcast_add_fusion.13
  525.1 1.7 bitcast_add_fusion.13
  526.8 1.7 bitcast_add_fusion.13
  528.5 1.7 bitcast_add_fusion.13
  530.2 1.7 bitcast_add_fusion.13
  532.0 1.7 bitcast_add_fusion.13
  533.7 1.7 bitcast_add_fusion.13
  535.4 1.7 bitcast_add_fusion.13
  537.1 1.7 bitcast_add_fusion.13
  538.9 1.7 bitcast_add_fusion.13
  540.6 1.7 bitcast_add_fusion.13
  542.3 1.7 bitcast_add_fusion.13
  544.0 1.7 bitcast_add_fusion.13
  545.8 1.7 bitcast_add_fusion.13
  554.4 1.7 bitcast_add_fusion.13
  557.9 1.7 bitcast_add_fusion.13
  561.3 1.7 bitcast_add_fusion.13
  564.8 1.7 bitcast_add_fusion.13
  568.2 1.7 bitcast_add_fusion.13
  571.7 1.7 bitcast_add_fusion.13
  575.1 1.7 bitcast_add_fusion.13
  578.6 1.7 bitcast_add_fusion.13
  587.2 1.7 bitcast_add_fusion.13
  590.6 1.7 bitcast_add_fusion.13
  594.1 1.7 bitcast_add_fusion.13
  605.0 5.9 fusion.151
  621.6 144.6 %all-gather.13.cloned.1.call-done = f32[2048,32,64]{2,1,0:T(8,128)} async-done(((f32[32,32,64]{2,1,0:T(8,128)}), f32[2048,32,64]{2,1,0:T(8,128)}) %all-gather.13.cloned.1.call-update) | async-done | bytes 16777232 | tf_op jit(solution)/shard_map/all_gather | solution.py:24
  766.2 142.2 %all-gather.11.cloned.1.call-done = f32[2048,32,64]{2,1,0:T(8,128)} async-done(((f32[32,32,64]{2,1,0:T(8,128)}), f32[2048,32,64]{2,1,0:T(8,128)}) %all-gather.11.cloned.1.call-update) | async-done | bytes 16777232 | tf_op jit(solution)/shard_map/all_gather | solution.py:24
  908.5 38.5 %while.32 = (s32[]{:T(128)}, f32[32,32,64]{2,1,0:T(8,128)S(1)}, f32[32,32,64]{2,1,0:T(8,128)S(1)}, s32[]{:T(128)}, f32[64,32]{1,0:T(8,128)}, /*index=5*/f32[64,3...) while((s32[]{:T(128)}, f32[32,32,64]{2,1,0:T(8,128)S(1)}, ...), condition=%wide.region_3.4_spmd, body=%wide.region_2.3_spmd.sunk | while | flops 393221 | bytes 1573783 | solution.py:33
  951.2 1.8 convolution_bitcast_fusion.5
  961.0 2.3 fusion.43
  963.3 2.3 fusion.51
  965.6 373.2 %all-reduce.21.cloned.1.call-done = (f32[2048,128]{1,0:T(8,128)}, f32[2048,32]{0,1:T(8,128)}, f32[2048,128]{1,0:T(8,128)}, f32[2048,32]{0,1:T(8,128)}) async-done(((f32[2048,128]{1,0:T(8,128)}, f32[2048,32]{0,1:T(8,128)}, f32[2048,128]{1,0:T(8,128)}, f32[2048,32]{0,1:T(8,128)}), (f32[2048,128]{1,0:T(8,128)}, f32[2048,32]{0,1:T(8,128)}, f32[2048,128]{1,0:T(8,128)}, ...) | async-done | bytes 2621456
  (285 shorter events, 111.1 us)
Async XLA Ops:
  7.2 220.9 %copy-start = (bf16[1,128,2048]{2,1,0:T(8,128)(2,1)S(1)}, bf16[1,128,2048]{2,1,0:T(8,128)(2,1)}, u32[]{:S(2)}) copy-start(bf16[1,128,2048]{2,1,0:T(8,128)(2,1)} %param.14) | copy-start | bytes 1572868
  7.2 155.0 %copy-start.43 = (f32[4,128]{1,0:T(4,128)S(1)}, f32[4,128]{1,0:T(4,128)}, u32[]{:S(2)}) copy-start(f32[4,128]{1,0:T(4,128)} %param.21) | copy-start | bytes 6148
  7.2 155.0 %copy-start.40 = (bf16[8,32]{1,0:T(8,128)(2,1)S(1)}, bf16[8,32]{1,0:T(8,128)(2,1)}, u32[]{:S(2)}) copy-start(bf16[8,32]{1,0:T(8,128)(2,1)} %param.20) | copy-start | bytes 1540
  7.2 220.7 %copy-start.12 = (bf16[1,128,1024]{2,1,0:T(8,128)(2,1)S(1)}, bf16[1,128,1024]{2,1,0:T(8,128)(2,1)}, u32[]{:S(2)}) copy-start(bf16[1,128,1024]{2,1,0:T(8,128)(2,1)} %param.16) | copy-start | bytes 786436
  8.0 220.0 %collective-permute-start = (bf16[3,2048]{1,0:T(4,128)(2,1)S(1)}, bf16[3,2048]{1,0:T(4,128)(2,1)S(1)}, u32[]{:S(2)}, u32[]{:S(2)}) collective-permute-start(bf16[3,2048]{1,0:T(4,128)(2,1)S(1)} %slice_bitcast_fusion), channel_id=1, source_target_pairs={{0,1},{1,2},{2,3},{3,4},{4,5},{5,6},{6,7},{7,8},{8,9},{9,10},{10,1... | collective-permute-start | bytes 36872 | tf_op jit(solution)/shard_map/ppermute | solution.py:17
  11.7 218.1 %all-to-all-start = ((bf16[256,2,128]{2,1,0:T(2,128)(2,1)}), bf16[256,2,128]{2,1,0:T(2,128)(2,1)S(1)}, u32[]{:S(2)}, u32[]{:S(2)}) async-start(bf16[256,2,128]{2,1,0:T(2,128)(2,1)} %reshape.135), calls=%async_computation | async-start | bytes 262144 | tf_op jit(solution)/shard_map/all_to_all | solution.py:103
  27.0 345.2 %all-gather.17.cloned.1.call-start = ((), (), s32[]{:S(2)}) async-start(), calls=%async_computation.4 | async-start | bytes 34078720 | tf_op jit(solution)/shard_map/all_gather | solution.py:24
  162.2 66.6 %copy-start.32 = (f32[128]{0:T(128)}, f32[128]{0:T(128)S(1)}, u32[]{:S(2)}) copy-start(f32[128]{0:T(128)S(1)} %get-tuple-element.319) | copy-start | bytes 1540
  162.2 66.6 %copy-start.34 = (f32[128]{0:T(128)}, f32[128]{0:T(128)S(1)}, u32[]{:S(2)}) copy-start(f32[128]{0:T(128)S(1)} %get-tuple-element.321) | copy-start | bytes 1540
  162.2 66.6 %copy-start.36 = (f32[128]{0:T(128)}, f32[128]{0:T(128)S(1)}, u32[]{:S(2)}) copy-start(f32[128]{0:T(128)S(1)} %get-tuple-element.322) | copy-start | bytes 1540
  162.3 66.6 %copy-start.38 = (f32[128]{0:T(128)}, f32[128]{0:T(128)S(1)}, u32[]{:S(2)}) copy-start(f32[128]{0:T(128)S(1)} %get-tuple-element.320) | copy-start | bytes 1540
  230.7 373.9 %copy-start.1 = (f32[128,32]{1,0:T(8,128)}, f32[128,32]{1,0:T(8,128)S(1)}, u32[]{:S(2)}) copy-start(f32[128,32]{1,0:T(8,128)S(1)} %get-tuple-element.326) | copy-start | bytes 49156
  231.0 3.6 copy-start.8
  233.2 281.4 %all-gather.15.cloned.1.call-start = ((), (), s32[]{:S(2)}) async-start(), calls=%async_computation.3 | async-start | bytes 34078720 | tf_op jit(solution)/shard_map/all_gather | solution.py:24
  234.6 531.5 %all-gather.13.cloned.1.call-start = ((), (), s32[]{:S(2)}) async-start(), calls=%async_computation.2 | async-start | bytes 34078720 | tf_op jit(solution)/shard_map/all_gather | solution.py:24
  234.9 363.1 %copy-start.26 = (f32[32]{0:T(128)}, f32[32]{0:T(128)S(1)}, u32[]{:S(2)}) copy-start(f32[32]{0:T(128)S(1)} %get-tuple-element.314) | copy-start | bytes 388
  234.9 363.1 %copy-start.30 = (f32[32]{0:T(128)}, f32[32]{0:T(128)S(1)}, u32[]{:S(2)}) copy-start(f32[32]{0:T(128)S(1)} %get-tuple-element.312) | copy-start | bytes 388
  597.9 5.8 copy-start.5
  602.2 306.1 %all-gather.11.cloned.1.call-start = ((), (), s32[]{:S(2)}) async-start(), calls=%async_computation.1 | async-start | bytes 34078720 | tf_op jit(solution)/shard_map/all_gather | solution.py:24
  603.6 735.2 %all-reduce.21.cloned.1.call-start = ((), (), s32[]{:S(2)}) async-start(), calls=%async_computation.5 | async-start | bytes 5242880
  610.9 297.5 %copy-start.3 = (f32[128,128]{1,0:T(8,128)}, f32[128,128]{1,0:T(8,128)S(1)}, u32[]{:S(2)}) copy-start(f32[128,128]{1,0:T(8,128)S(1)} %get-tuple-element.236) | copy-start | bytes 196612
  949.6 3.4 copy-start.41
  949.6 3.4 copy-start.42
  949.7 3.4 copy-start.44
  949.7 3.4 copy-start.45
  949.7 3.4 copy-start.9
  949.7 3.4 copy-start.16
  949.7 3.4 copy-start.17
  949.7 3.4 copy-start.18
  949.7 3.4 copy-start.19
  949.7 3.4 copy-start.20
  949.7 3.4 copy-start.27
  951.2 4.3 copy-start.4
  953.0 5.0 copy-start.7
  953.0 5.0 copy-start.29
  953.3 5.9 copy-start.2
  953.3 5.9 copy-start.6
  953.3 5.9 copy-start.13
  953.3 5.9 copy-start.31
  954.4 6.0 copy-start.23
  954.4 6.3 copy-start.11
  954.4 6.3 copy-start.15
  954.4 6.3 copy-start.21
  954.5 6.3 copy-start.22
  954.5 6.3 copy-start.39
  955.5 5.3 copy-start.33
  955.5 5.3 copy-start.35
  955.5 5.3 copy-start.37
  (6 other events, 10.0 us)
Sparse Core Ops, SparseCore 0:
  233.3 138.8 all-gather.16
  375.0 139.4 all-gather.14
  602.3 163.8 all-gather.12
  768.8 139.4 all-gather.10
  965.7 373.0 all-reduce.20
